TPU v7x, 32 devices: a whole 2x2x4 slice. The times are simulated.
32 devices in a mesh: req: 4 (over y, x), grp: 8 (over z, core).
Axes of the slice: x: 2, y: 2, z: 4, core: 2. Of those that a mesh axis runs over, the one named last changes fastest.
Arguments:
- item_table: bfloat16 [32768, 512], P('grp'), may hold values from -6 to 6
- cand_owner: int32 [4, 8192, 1], P('req', 'grp'), may hold values from 0 to 7; in each aligned block of 1024 rows (0 to 1023, 1024 to 2047, ..., all dimensions but the last counted through in order) at most 128 rows name the same one
- cand_row: int32 [4, 8192], P('req', 'grp'), may hold values from 0 to 4095
- hist_kv: bfloat16 [2, 4, 2048, 1024], P(None, 'req', 'grp'), may hold values from -6 to 6
- hist_len: int32 [4], P('req'), may hold values from 512 to 2048, as said below
- w_in: bfloat16 [2, 512, 1024], replicated, may hold values from -0.25 to 0.25
- w_out: bfloat16 [2, 512, 512], replicated, may hold values from -0.25 to 0.25
Outputs:
- candidate_states: bfloat16 [4, 8192, 512], P('req', 'grp')
Inputs may be any that keep to these rules, and one draw needn't show every extreme that they name: `cand_owner`: among the 1024 candidates of one device, at most 128 name the same block, and some block is named exactly 128 times. `hist_len`: some request has all 2048 events live.
All inputs are finite; a program needn't handle non-finite values.
Results may differ from a plain program's by a relative error of at most 0.0085.
Values may be sent and summed in bfloat16 or wider, within the bound.
A program may use at most 128 MiB of HBM per device.

v0:
```python
from functools import partial
import math

import jax
import jax.numpy as jnp
from jax import lax
from jax.sharding import PartitionSpec as P

D = 512
HEADS = 4
HEAD = 128
LAYERS = 2
MOST = 128


score_scale = 0.35
epsilon = 1e-05


def normalize(values):
    center = values - jnp.mean(values, axis=-1, keepdims=True)
    return center * lax.rsqrt(jnp.mean(center * center, axis=-1, keepdims=True) + epsilon)


def attend_rows(running, cache_piece, offset, queries, length):
    piece_rows = cache_piece.shape[0]
    block_rows = math.gcd(piece_rows, 512)
    cand_rows = queries.shape[0]

    def step(block_index, summed):
        part_rows = lax.dynamic_slice_in_dim(cache_piece, block_index * block_rows, block_rows, 0)
        key_rows = part_rows[:, :D].reshape(block_rows, HEADS, HEAD)
        value_rows = part_rows[:, D:].reshape(block_rows, HEADS, HEAD)
        scores = (
            jnp.einsum("chd,khd->hck", queries, key_rows, preferred_element_type=jnp.float32)
            * score_scale
        )
        position = block_index * block_rows + jnp.arange(block_rows, dtype=jnp.int32)
        weights = jnp.where(position[None, None, :] < length, jax.nn.silu(scores), 0.0).astype(
            jnp.bfloat16
        )
        attended = jnp.einsum(
            "hck,khd->chd", weights, value_rows, preferred_element_type=jnp.float32
        )
        return summed + attended.reshape(cand_rows, D)

    return lax.fori_loop(0, piece_rows // block_rows, step, running)


def hstu_layer(rows_now, weight_in, weight_out, attend_fn):
    normed = normalize(rows_now.astype(jnp.float32)).astype(jnp.bfloat16)
    projected = jax.nn.silu(jnp.dot(normed, weight_in, preferred_element_type=jnp.float32))
    gate_vals = projected[:, :D]
    queries = projected[:, D:].astype(jnp.bfloat16).reshape(rows_now.shape[0], HEADS, HEAD)
    attended = attend_fn(queries)
    hidden = (normalize(attended) * gate_vals).astype(jnp.bfloat16)
    return (
        rows_now.astype(jnp.float32)
        + jnp.dot(hidden, weight_out, preferred_element_type=jnp.float32)
    ).astype(jnp.bfloat16)


def body(item_table, cand_owner, cand_row, hist_kv, hist_len, w_in, w_out):
    groups = lax.axis_size("grp")
    owners = cand_owner[0, :, 0]
    item_rows = cand_row[0]
    one_hot = (owners[:, None] == jnp.arange(groups, dtype=jnp.int32)[None, :]).astype(jnp.int32)
    slot_index = jnp.sum((jnp.cumsum(one_hot, axis=0) - 1) * one_hot, axis=1)
    flat_index = owners * MOST + slot_index
    requested = (
        jnp.zeros((groups * MOST,), jnp.int32).at[flat_index].set(item_rows).reshape(groups, MOST)
    )
    wanted = lax.all_to_all(requested, "grp", split_axis=0, concat_axis=0, tiled=True)
    wanted_flat = wanted.reshape(-1)
    found = jnp.take(item_table, wanted_flat, axis=0)
    found = found.reshape(wanted.shape[0], wanted.shape[1], D)
    returned = lax.all_to_all(found, "grp", split_axis=0, concat_axis=0, tiled=True)
    rows_now = returned.reshape(groups * MOST, D)[flat_index]
    length = hist_len[0]
    for layer_index in range(LAYERS):
        empty = jnp.zeros((rows_now.shape[0], D), jnp.float32)

        def attend_fn(queries, layer_index=layer_index, empty=empty):
            folder = partial(attend_rows, queries=queries, length=length)
            return folder(
                empty,
                lax.all_gather(hist_kv[layer_index, 0], "grp", axis=0, tiled=True),
                jnp.int32(0),
            )

        rows_now = hstu_layer(rows_now, w_in[layer_index], w_out[layer_index], attend_fn)
    return rows_now[None]


def solution(mesh):
    in_specs = (
        P("grp", None),
        P("req", "grp", None),
        P("req", "grp"),
        P(None, "req", "grp", None),
        P("req"),
        P(),
        P(),
    )
    out_specs = P("req", "grp", None)
    return jax.shard_map(body, mesh=mesh, in_specs=in_specs, out_specs=out_specs, check_vma=False)
```

profile of v0, /device:TPU:0, one launch (start us, length us, event | category | flops | bytes accessed | tf_op | source)
XLA Modules:
  0.0 206.5 jit_solution(17276218383037527179)
XLA Ops:
  6.5 1.3 fusion.62
  7.8 1.0 copy.44
  8.9 2.3 %reduce-window.6 = s32[8,8,128]{2,1,0:T(8,128)S(1)} reduce-window(s32[8,8,128]{2,1,0:T(8,128)S(1)} %fusion.59, s32[]{:T(128)} %constant.130.clone.1), window={size=1x1x128 pad=0_0x0_0x127_0}, to_apply=%region_0.0 | reduce-window | flops 1040384 | bytes 65540 | tf_op jit(solution)/shard_map/reduce-window
  11.7 4.5 %scatter_custom_fusion = s32[1024]{0:T(1024)S(1)} fusion(s32[1024]{0:T(1024)S(1)} %bitcast.144, s32[1024]{0:T(1024)} %bitcast.149, s32[]{:T(128)} %constant.130.clone.1), kind=kCustom, calls=%fused_computation.100 | custom fusion | bytes 4608 | tf_op jit(solution)/shard_map/scatter | solution.py:71
  16.2 13.4 %all_to_all.14 = s32[8,1,128]{2,1,0:T(1,128)S(1)} all-to-all(s32[8,1,128]{2,1,0:T(1,128)S(1)} %bitcast.147), channel_id=1, replica_groups=mesh['req'=4,'grp'=8] {'grp'}, dimensions={0} | all-to-all | bytes 8192 | tf_op jit(solution)/shard_map/all_to_all | solution.py:73
  29.6 6.8 %gather_fusion = bf16[1024,512]{1,0:T(8,128)(2,1)S(1)} fusion(bf16[4096,512]{1,0:T(8,128)(2,1)} %param.11, s32[1024]{0:T(1024)S(1)} %broadcast_clamp_fusion.1), kind=kCustom, calls=%fused_computation | custom fusion | bytes 2101248 | tf_op jit(solution)/shard_map/jit(_take)/gather | solution.py:75
  36.4 1.2 broadcast_select_fusion
  37.6 3.6 %all-to-all-start.1 = ((bf16[8,128,512]{2,1,0:T(8,128)(2,1)}), bf16[8,128,512]{2,1,0:T(8,128)(2,1)S(1)}, u32[]{:S(2)}, u32[]{:S(2)}) async-start(bf16[8,128,512]{2,1,0:T(8,128)(2,1)} %broadcast_select_fusion), calls=%async_computation.1 | async-start | bytes 2097152 | tf_op jit(solution)/shard_map/all_to_all | solution.py:77
  41.4 1.0 copy.45
  42.5 37.8 %all-to-all-done.1 = bf16[8,128,512]{2,1,0:T(8,128)(2,1)S(1)} async-done(((bf16[8,128,512]{2,1,0:T(8,128)(2,1)}), bf16[8,128,512]{2,1,0:T(8,128)(2,1)S(1)}, u32[]{:S(2)}, u32[]{:S(2)}) %all-to-all-start.1) | async-done | bytes 1048608 | tf_op jit(solution)/shard_map/all_to_all | solution.py:77
  80.3 5.1 %gather_fusion.1 = bf16[1024,512]{1,0:T(8,128)(2,1)} fusion(bf16[1024,512]{1,0:T(8,128)(2,1)S(1)} %bitcast.130, s32[1024]{0:T(1024)S(1)} %broadcast_clamp_fusion), kind=kCustom, calls=%fused_computation.1 | custom fusion | bytes 2101248 | tf_op jit(solution)/shard_map/gather | solution.py:78
  85.3 1.6 copy.32
  87.2 0.3 fusion.30
  87.5 1.1 copy-done.8
  88.6 1.9 divide_multiply_fusion.1
  90.6 2.0 copy-done.3
  92.5 1.1 slice.119
  93.7 2.3 %copy.34 = bf16[1024,4,128]{2,0,1:T(8,128)(2,1)} copy(bf16[1024,4,128]{0,2,1:T(8,128)(2,1)} %bitcast.138) | data formatting | bytes 2097152
  95.9 46.0 %while.28 = (s32[]{:T(128)}, f32[1024,512]{0,1:T(8,128)S(1)}, bf16[2048,1024]{0,1:T(8,128)(2,1)}, s32[]{:T(128)}, bf16[1024,4,128]{2,0,1:T(8,128)(2,1)}, /*index...) while((s32[]{:T(128)}, f32[1024,512]{0,1:T(8,128)S(1)}, bf16[2048,1024]{0,1:T(8,128)(2,1)}, ...), condition=%wide.region_7.8_spmd.clone, body=%wide.region_6.7_spmd.clone.sunk | while | flops 1089471488 | bytes 12584121 | solution.py:47
  95.9 2.3 %constant_dynamic-slice_fusion.4 = (bf16[512,512]{0,1:T(8,128)(2,1)}, bf16[512,512]{0,1:T(8,128)(2,1)}) fusion(bf16[2048,1024]{0,1:T(8,128)(2,1)} %get-tuple-element.381, s32[]{:T(128)S(6)} %select_n.89, s32[]{:T(128)S(6)} %add.297), kind=kLoop, calls=%fused_computation.14.clone.1 | loop fusion | bytes 2097160 | tf_op jit(solution)/shard_map/while/body/eval_jaxpr/slice | solution.py:32
  98.2 0.7 add_compare_fusion.4
  98.9 6.2 %fusion.83 = f32[4,128,1024]{2,1,0:T(8,128)} fusion(bf16[512,4,128]{0,2,1:T(8,128)(2,1)} %bitcast.132, pred[512]{0:T(512)(128)(4,1)S(1)} %add_compare_fusion.4, bf16[512,4,128]{0,2,1:T(8,128)(2,1)} %bitcast.131, bf16[1024,4,128]{2,0,1:T(8,128)(2,1)} %get-tuple-element.383), kind=kOutput, calls=%fused_computation.10.clone.1 | convolution fusion | flops 1088421888 | bytes 4194816 | tf_op jit(solution)/shard_map/while/body/eval_jaxpr/hck,khd->chd/dot_general | solution.py:42
  105.1 2.3 %bitcast_add_fusion.5 = f32[1024,512]{0,1:T(8,128)S(1)} fusion(f32[4,128,1024]{2,1,0:T(8,128)} %fusion.83, f32[1024,512]{0,1:T(8,128)S(1)} %get-tuple-element.370, pred[]{:T(512)S(6)} %compare.6), kind=kLoop, calls=%fused_computation.12.clone.1 | loop fusion | flops 1048576 | bytes 6291457 | tf_op jit(solution)/shard_map/while/body/eval_jaxpr/add | solution.py:45
  107.4 2.3 %constant_dynamic-slice_fusion.4 = (bf16[512,512]{0,1:T(8,128)(2,1)}, bf16[512,512]{0,1:T(8,128)(2,1)}) fusion(bf16[2048,1024]{0,1:T(8,128)(2,1)} %get-tuple-element.381, s32[]{:T(128)S(6)} %select_n.89, s32[]{:T(128)S(6)} %add.297), kind=kLoop, calls=%fused_computation.14.clone.1 | loop fusion | bytes 2097160 | tf_op jit(solution)/shard_map/while/body/eval_jaxpr/slice | solution.py:32
  109.7 0.7 add_compare_fusion.4
  110.4 6.3 %fusion.83 = f32[4,128,1024]{2,1,0:T(8,128)} fusion(bf16[512,4,128]{0,2,1:T(8,128)(2,1)} %bitcast.132, pred[512]{0:T(512)(128)(4,1)S(1)} %add_compare_fusion.4, bf16[512,4,128]{0,2,1:T(8,128)(2,1)} %bitcast.131, bf16[1024,4,128]{2,0,1:T(8,128)(2,1)} %get-tuple-element.383), kind=kOutput, calls=%fused_computation.10.clone.1 | convolution fusion | flops 1088421888 | bytes 4194816 | tf_op jit(solution)/shard_map/while/body/eval_jaxpr/hck,khd->chd/dot_general | solution.py:42
  116.6 2.3 %bitcast_add_fusion.5 = f32[1024,512]{0,1:T(8,128)S(1)} fusion(f32[4,128,1024]{2,1,0:T(8,128)} %fusion.83, f32[1024,512]{0,1:T(8,128)S(1)} %get-tuple-element.370, pred[]{:T(512)S(6)} %compare.6), kind=kLoop, calls=%fused_computation.12.clone.1 | loop fusion | flops 1048576 | bytes 6291457 | tf_op jit(solution)/shard_map/while/body/eval_jaxpr/add | solution.py:45
  119.0 2.3 %constant_dynamic-slice_fusion.4 = (bf16[512,512]{0,1:T(8,128)(2,1)}, bf16[512,512]{0,1:T(8,128)(2,1)}) fusion(bf16[2048,1024]{0,1:T(8,128)(2,1)} %get-tuple-element.381, s32[]{:T(128)S(6)} %select_n.89, s32[]{:T(128)S(6)} %add.297), kind=kLoop, calls=%fused_computation.14.clone.1 | loop fusion | bytes 2097160 | tf_op jit(solution)/shard_map/while/body/eval_jaxpr/slice | solution.py:32
  121.2 0.7 add_compare_fusion.4
  121.9 6.2 %fusion.83 = f32[4,128,1024]{2,1,0:T(8,128)} fusion(bf16[512,4,128]{0,2,1:T(8,128)(2,1)} %bitcast.132, pred[512]{0:T(512)(128)(4,1)S(1)} %add_compare_fusion.4, bf16[512,4,128]{0,2,1:T(8,128)(2,1)} %bitcast.131, bf16[1024,4,128]{2,0,1:T(8,128)(2,1)} %get-tuple-element.383), kind=kOutput, calls=%fused_computation.10.clone.1 | convolution fusion | flops 1088421888 | bytes 4194816 | tf_op jit(solution)/shard_map/while/body/eval_jaxpr/hck,khd->chd/dot_general | solution.py:42
  128.1 2.3 %bitcast_add_fusion.5 = f32[1024,512]{0,1:T(8,128)S(1)} fusion(f32[4,128,1024]{2,1,0:T(8,128)} %fusion.83, f32[1024,512]{0,1:T(8,128)S(1)} %get-tuple-element.370, pred[]{:T(512)S(6)} %compare.6), kind=kLoop, calls=%fused_computation.12.clone.1 | loop fusion | flops 1048576 | bytes 6291457 | tf_op jit(solution)/shard_map/while/body/eval_jaxpr/add | solution.py:45
  130.4 2.3 %constant_dynamic-slice_fusion.4 = (bf16[512,512]{0,1:T(8,128)(2,1)}, bf16[512,512]{0,1:T(8,128)(2,1)}) fusion(bf16[2048,1024]{0,1:T(8,128)(2,1)} %get-tuple-element.381, s32[]{:T(128)S(6)} %select_n.89, s32[]{:T(128)S(6)} %add.297), kind=kLoop, calls=%fused_computation.14.clone.1 | loop fusion | bytes 2097160 | tf_op jit(solution)/shard_map/while/body/eval_jaxpr/slice | solution.py:32
  132.7 0.7 add_compare_fusion.4
  133.4 6.2 %fusion.83 = f32[4,128,1024]{2,1,0:T(8,128)} fusion(bf16[512,4,128]{0,2,1:T(8,128)(2,1)} %bitcast.132, pred[512]{0:T(512)(128)(4,1)S(1)} %add_compare_fusion.4, bf16[512,4,128]{0,2,1:T(8,128)(2,1)} %bitcast.131, bf16[1024,4,128]{2,0,1:T(8,128)(2,1)} %get-tuple-element.383), kind=kOutput, calls=%fused_computation.10.clone.1 | convolution fusion | flops 1088421888 | bytes 4194816 | tf_op jit(solution)/shard_map/while/body/eval_jaxpr/hck,khd->chd/dot_general | solution.py:42
  139.6 2.3 %bitcast_add_fusion.5 = f32[1024,512]{0,1:T(8,128)S(1)} fusion(f32[4,128,1024]{2,1,0:T(8,128)} %fusion.83, f32[1024,512]{0,1:T(8,128)S(1)} %get-tuple-element.370, pred[]{:T(512)S(6)} %compare.6), kind=kLoop, calls=%fused_computation.12.clone.1 | loop fusion | flops 1048576 | bytes 6291457 | tf_op jit(solution)/shard_map/while/body/eval_jaxpr/add | solution.py:45
  142.1 0.3 multiply_reduce_fusion.1
  142.4 0.9 copy-done.5
  143.3 2.5 %convert_reduce_fusion = (f32[1024]{0:T(1024)S(1)}, bf16[1024,512]{0,1:T(8,128)(2,1)S(1)}) fusion(bf16[2,512,512]{2,1,0:T(8,128)(2,1)S(1)} %copy-done.5, f32[1024,1024]{0,1:T(8,128)} %copy-done.3, f32[1024,512]{0,1:T(8,128)S(1)} %get-tuple-element.193, f32[1024]{0:T(1024)S(1)} %add_rsqrt_fusion.2, f32[1024]{0:T(1024)S(1)} %broadcast_multiply_fusion.2, ...), kind=kOutput, calls=%fused_computation.37 | convolution fusion | flops 541588480 | bytes 6828032 | tf_op jit(solution)/shard_map/dot_general | solution.py:59
  145.9 0.3 fusion.28
  146.2 1.9 divide_multiply_fusion
  148.3 2.0 copy-done.4
  150.3 1.3 copy.36
  151.6 40.9 %while.29 = (s32[]{:T(128)}, f32[1024,512]{0,1:T(8,128)S(1)}, bf16[2048,1024]{0,1:T(8,128)(2,1)}, s32[]{:T(128)}, bf16[1024,4,128]{2,0,1:T(8,128)(2,1)}, /*index...) while((s32[]{:T(128)}, f32[1024,512]{0,1:T(8,128)S(1)}, bf16[2048,1024]{0,1:T(8,128)(2,1)}, ...), condition=%wide.region_13.14_spmd.clone, body=%wide.region_12.13_spmd.clone.sunk | while | flops 1089471488 | bytes 12584121 | solution.py:47
  151.6 1.3 constant_dynamic-slice_fusion.5
  152.9 0.7 add_compare_fusion.5
  153.5 6.0 %fusion.88 = f32[4,128,1024]{2,1,0:T(8,128)} fusion(bf16[512,4,128]{0,2,1:T(8,128)(2,1)S(1)} %bitcast.134, pred[512]{0:T(512)(128)(4,1)S(1)} %add_compare_fusion.5, bf16[512,4,128]{0,2,1:T(8,128)(2,1)S(1)} %bitcast.133, bf16[1024,4,128]{2,0,1:T(8,128)(2,1)} %get-tuple-element.413), kind=kOutput, calls=%fused_computation.25.clone.1 | convolution fusion | flops 1088421888 | bytes 4194816 | tf_op jit(solution)/shard_map/while/body/eval_jaxpr/hck,khd->chd/dot_general | solution.py:42
  159.5 2.3 %bitcast_add_fusion.6 = f32[1024,512]{0,1:T(8,128)S(1)} fusion(f32[4,128,1024]{2,1,0:T(8,128)} %fusion.88, f32[1024,512]{0,1:T(8,128)S(1)} %get-tuple-element.400, pred[]{:T(512)S(6)} %compare.7), kind=kLoop, calls=%fused_computation.27.clone.1 | loop fusion | flops 1048576 | bytes 6291457 | tf_op jit(solution)/shard_map/while/body/eval_jaxpr/add | solution.py:45
  161.8 1.3 constant_dynamic-slice_fusion.5
  163.1 0.7 add_compare_fusion.5
  163.8 6.0 %fusion.88 = f32[4,128,1024]{2,1,0:T(8,128)} fusion(bf16[512,4,128]{0,2,1:T(8,128)(2,1)S(1)} %bitcast.134, pred[512]{0:T(512)(128)(4,1)S(1)} %add_compare_fusion.5, bf16[512,4,128]{0,2,1:T(8,128)(2,1)S(1)} %bitcast.133, bf16[1024,4,128]{2,0,1:T(8,128)(2,1)} %get-tuple-element.413), kind=kOutput, calls=%fused_computation.25.clone.1 | convolution fusion | flops 1088421888 | bytes 4194816 | tf_op jit(solution)/shard_map/while/body/eval_jaxpr/hck,khd->chd/dot_general | solution.py:42
  169.7 2.3 %bitcast_add_fusion.6 = f32[1024,512]{0,1:T(8,128)S(1)} fusion(f32[4,128,1024]{2,1,0:T(8,128)} %fusion.88, f32[1024,512]{0,1:T(8,128)S(1)} %get-tuple-element.400, pred[]{:T(512)S(6)} %compare.7), kind=kLoop, calls=%fused_computation.27.clone.1 | loop fusion | flops 1048576 | bytes 6291457 | tf_op jit(solution)/shard_map/while/body/eval_jaxpr/add | solution.py:45
  172.1 1.3 constant_dynamic-slice_fusion.5
  173.3 0.7 add_compare_fusion.5
  174.0 6.0 %fusion.88 = f32[4,128,1024]{2,1,0:T(8,128)} fusion(bf16[512,4,128]{0,2,1:T(8,128)(2,1)S(1)} %bitcast.134, pred[512]{0:T(512)(128)(4,1)S(1)} %add_compare_fusion.5, bf16[512,4,128]{0,2,1:T(8,128)(2,1)S(1)} %bitcast.133, bf16[1024,4,128]{2,0,1:T(8,128)(2,1)} %get-tuple-element.413), kind=kOutput, calls=%fused_computation.25.clone.1 | convolution fusion | flops 1088421888 | bytes 4194816 | tf_op jit(solution)/shard_map/while/body/eval_jaxpr/hck,khd->chd/dot_general | solution.py:42
  180.0 2.3 %bitcast_add_fusion.6 = f32[1024,512]{0,1:T(8,128)S(1)} fusion(f32[4,128,1024]{2,1,0:T(8,128)} %fusion.88, f32[1024,512]{0,1:T(8,128)S(1)} %get-tuple-element.400, pred[]{:T(512)S(6)} %compare.7), kind=kLoop, calls=%fused_computation.27.clone.1 | loop fusion | flops 1048576 | bytes 6291457 | tf_op jit(solution)/shard_map/while/body/eval_jaxpr/add | solution.py:45
  182.3 1.3 constant_dynamic-slice_fusion.5
  183.6 0.7 add_compare_fusion.5
  184.2 6.0 %fusion.88 = f32[4,128,1024]{2,1,0:T(8,128)} fusion(bf16[512,4,128]{0,2,1:T(8,128)(2,1)S(1)} %bitcast.134, pred[512]{0:T(512)(128)(4,1)S(1)} %add_compare_fusion.5, bf16[512,4,128]{0,2,1:T(8,128)(2,1)S(1)} %bitcast.133, bf16[1024,4,128]{2,0,1:T(8,128)(2,1)} %get-tuple-element.413), kind=kOutput, calls=%fused_computation.25.clone.1 | convolution fusion | flops 1088421888 | bytes 4194816 | tf_op jit(solution)/shard_map/while/body/eval_jaxpr/hck,khd->chd/dot_general | solution.py:42
  190.2 2.3 %bitcast_add_fusion.6 = f32[1024,512]{0,1:T(8,128)S(1)} fusion(f32[4,128,1024]{2,1,0:T(8,128)} %fusion.88, f32[1024,512]{0,1:T(8,128)S(1)} %get-tuple-element.400, pred[]{:T(512)S(6)} %compare.7), kind=kLoop, calls=%fused_computation.27.clone.1 | loop fusion | flops 1048576 | bytes 6291457 | tf_op jit(solution)/shard_map/while/body/eval_jaxpr/add | solution.py:45
  192.7 0.3 multiply_reduce_fusion
  193.0 0.7 copy-done.2
  193.7 0.4 copy-done.6
  194.1 3.4 %fusion.36 = bf16[1,1024,512]{1,2,0:T(8,128)(2,1)} fusion(bf16[1024,512]{0,1:T(8,128)(2,1)S(1)} %copy-done.2, f32[1024,1024]{0,1:T(8,128)} %copy-done.4, f32[1024,512]{0,1:T(8,128)S(1)} %get-tuple-element.194, f32[1024]{0:T(1024)S(1)} %add_rsqrt_fusion, f32[1024]{0:T(1024)S(1)} %broadcast_multiply_fusion, bf16[2,512,512]{2,1,0:T(8,128)(2,1)S(1)} %copy-done.6), kind=kOutput, calls=%fused_computation.59 | convolution fusion | flops 540540928 | bytes 6823936 | tf_op jit(solution)/shard_map/dot_general | solution.py:59
  197.4 2.3 %copy.38 = bf16[1,1024,512]{2,1,0:T(8,128)(2,1)} copy(bf16[1,1024,512]{1,2,0:T(8,128)(2,1)} %fusion.36) | data formatting | bytes 2097152 | tf_op jit(solution)/shard_map/broadcast_in_dim | solution.py:92
  (44 shorter events, 1.6 us)
Async XLA Ops:
  6.5 2.3 %copy-start.7 = (s32[1,1024,1]{1,2,0:T(1,128)S(1)}, s32[1,1024,1]{1,2,0:T(1,128)}, u32[]{:S(2)}) copy-start(s32[1,1024,1]{1,2,0:T(1,128)} %param.12) | copy-start | bytes 12292
  6.5 89.4 %all-gather.5.cloned.1.call-start = ((), (), s32[]{:S(2)}) async-start(), calls=%async_computation.2 | async-start | bytes 4718592 | tf_op jit(solution)/shard_map/all_gather | solution.py:87
  37.6 42.7 %all-to-all-start.1 = ((bf16[8,128,512]{2,1,0:T(8,128)(2,1)}), bf16[8,128,512]{2,1,0:T(8,128)(2,1)S(1)}, u32[]{:S(2)}, u32[]{:S(2)}) async-start(bf16[8,128,512]{2,1,0:T(8,128)(2,1)} %broadcast_select_fusion), calls=%async_computation.1 | async-start | bytes 2097152 | tf_op jit(solution)/shard_map/all_to_all | solution.py:77
  41.1 110.4 %all-gather.7.cloned.1.call-start = ((), (), s32[]{:S(2)}) async-start(), calls=%async_computation.3 | async-start | bytes 4718592 | tf_op jit(solution)/shard_map/all_gather | solution.py:87
  87.0 1.6 copy-start.8
  90.5 2.0 copy-start.3
  142.1 1.2 copy-start.5
  143.3 2.9 %copy-start.9 = (bf16[2,512,1024]{2,1,0:T(8,128)(2,1)S(1)}, bf16[2,512,1024]{2,1,0:T(8,128)(2,1)}, u32[]{:S(2)}) copy-start(bf16[2,512,1024]{2,1,0:T(8,128)(2,1)} %param.16) | copy-start | bytes 6291460
  145.8 2.3 %copy-start.1 = (bf16[1024,512]{0,1:T(8,128)(2,1)}, bf16[1024,512]{0,1:T(8,128)(2,1)S(1)}, u32[]{:S(2)}) copy-start(bf16[1024,512]{0,1:T(8,128)(2,1)S(1)} %get-tuple-element.288) | copy-start | bytes 3145732
  148.1 2.1 %copy-start.4 = (f32[1024,1024]{0,1:T(8,128)}, f32[1024,1024]{0,1:T(8,128)S(1)}, u32[]{:S(2)}) copy-start(f32[1024,1024]{0,1:T(8,128)S(1)} %divide_multiply_fusion) | copy-start | bytes 12582916
  148.2 3.4 %copy-start = (f32[1024,512]{0,1:T(8,128)S(1)}, f32[1024,512]{0,1:T(8,128)}, u32[]{:S(2)}) copy-start(f32[1024,512]{0,1:T(8,128)} %custom-call.1) | copy-start | bytes 6291460
  192.5 1.2 copy-start.2
  192.7 1.4 copy-start.6
Sparse Core Ops, SparseCore 0:
  9.0 69.4 all-gather.4
  80.1 45.2 all-gather.6
where the time goes:
time: 208 us; the launch traced here: 207 us
  matrix products  58.5 us (28%)
  local copies, waits for them, and re-layouts  49.9 us (24%)
  waiting for transfers between devices  37.8 us (18%)
  other arithmetic  29.2 us (14%)
  between operations  13.7 us (7%)
  blocking collectives  13.4 us (6%)
  starting transfers between devices  3.78 us (2%)
    dot_general x8, matrix products, step(): jnp.einsum('hck,khd->chd', weights, value_rows, preferred_element_type=jn...  48.8 us
    all_to_all x1, waiting for transfers between devices, body(): lax.all_to_all(found, 'grp', split_axis=0, concat_axis=0, tiled=True)  37.8 us
    add x8, other arithmetic, step(): return summed + attended.reshape(cand_rows, D)  18.5 us
    slice x8, local copies, waits for them, and re-layouts, step(): key_rows = part_rows[:, :D].reshape(block_rows, HEADS, HEAD)  14.2 us
    all_to_all x1, blocking collectives, body(): lax.all_to_all(requested, 'grp', split_axis=0, concat_axis=0, tiled=True)  13.4 us
    unnamed x24, local copies, waits for them, and re-layouts  12.7 us
    gather x1, local copies, waits for them, and re-layouts, body(): found = jnp.take(item_table, wanted_flat, axis=0)  6.76 us
    gather x2, local copies, waits for them, and re-layouts, body(): rows_now = returned.reshape(groups * MOST, D)[flat_index]  6.7 us
  transfers between devices with their start and end apart: 3, of which 1 were waited for; matrix products, arithmetic and copies ran while one was open for 39% of the time, Pallas kernels for 0%

commit v1 on v0

v1 whole, which is shorter than its diff:
```python
from functools import partial

import jax
import jax.numpy as jnp
from jax import lax
from jax.experimental import pallas as pl
from jax.experimental.pallas import tpu as pltpu
from jax.sharding import PartitionSpec as P

D = 512
HEADS = 4
HEAD = 128
LAYERS = 2
MOST = 128
MESH = pl.DeviceIdType.MESH

score_scale = 0.35
epsilon = 1e-05


def normalize(values):
    center = values - jnp.mean(values, axis=-1, keepdims=True)
    return center * lax.rsqrt(jnp.mean(center * center, axis=-1, keepdims=True) + epsilon)


def silu_of_twice(half):
    return half + half * jnp.tanh(half)


def kernel(
    groups,
    len_ref, owner_ref, row_ref, table_ref, hist_ref, w_in_ref, w_out_ref, out_ref,
    kv, place, asked, wanted, found, returned, rows_now, queries, gate, summed, live_values,
    own_sem, z_recv, s_recv, r_send, l_send, s_send, ask_send, ask_recv, back_send, back_recv,
):
    chips = groups // 2
    me = lax.axis_index("grp")
    pos, core = me // 2, me % 2
    sibling = 2 * pos + 1 - core
    cands = rows_now.shape[0]
    items = table_ref.shape[0]
    hist_rows = hist_ref.shape[1]
    tile = 256
    f32, bf16 = jnp.float32, jnp.bfloat16

    barrier = pltpu.get_barrier_semaphore()

    @pl.loop(1, groups)
    def _(k):
        pl.semaphore_signal(
            barrier, inc=1, device_id={"grp": (me + k) % groups}, device_id_type=MESH
        )

    own_copies = [
        pltpu.make_async_copy(hist_ref.at[layer], kv.at[layer, me], own_sem.at[layer])
        for layer in range(LAYERS)
    ]
    for copy in own_copies:
        copy.start()
    pl.semaphore_wait(barrier, groups - 1)

    def push(layer, chip, lane, target, send, recv):
        block = kv.at[layer, 2 * chip + lane]
        return pltpu.make_async_remote_copy(
            src_ref=block, dst_ref=block, send_sem=send.at[layer, chip],
            recv_sem=recv.at[layer, chip], device_id={"grp": target}, device_id_type=MESH,
        )

    def to_right(layer, chip):
        return push(layer, chip, core, me + 2, r_send, z_recv)

    def to_left(layer, chip):
        return push(layer, chip, core, me - 2, l_send, z_recv)

    def to_sibling(layer, chip):
        return push(layer, chip, core, sibling, s_send, s_recv)

    def from_sibling(layer, chip):
        return push(layer, chip, 1 - core, sibling, s_send, s_recv)

    def goes_right(chip):
        return jnp.logical_and(chip <= pos, pos + 1 < chips)

    def goes_left(chip):
        return jnp.logical_and(chip >= pos, pos > 0)

    def pass_on(layer, chip):
        @pl.when(goes_right(chip))
        def _():
            to_right(layer, chip).start()

        @pl.when(goes_left(chip))
        def _():
            to_left(layer, chip).start()

        to_sibling(layer, chip).start()

    def at_distance(distance, act):
        @pl.loop(0, 2)
        def _(side):
            chip = pos + (2 * side - 1) * distance

            @pl.when(jnp.logical_and(chip >= 0, chip < chips))
            def _():
                act(chip)

    def relay(layer, distance):
        def act(chip):
            to_right(layer, chip).wait_recv()
            pass_on(layer, chip)

        at_distance(distance, act)

    own_copies[0].wait()
    pass_on(0, pos)

    owners = owner_ref[...]
    names = (owners == lax.broadcasted_iota(jnp.int32, (cands, 128), 1)).astype(f32)
    names16 = names.astype(bf16)
    for start in range(0, cands, tile):
        earlier = (
            lax.broadcasted_iota(jnp.int32, (tile, cands), 1)
            < start + lax.broadcasted_iota(jnp.int32, (tile, cands), 0)
        ).astype(f32).astype(bf16)
        rank = jnp.dot(earlier, names16, preferred_element_type=f32)
        own_rank = jnp.sum(rank * names[start : start + tile], axis=1, keepdims=True)
        flat = owners[start : start + tile] * MOST + own_rank.astype(jnp.int32)
        place[start : start + tile, :] = (
            (flat == lax.broadcasted_iota(jnp.int32, (tile, groups * MOST), 1))
            .astype(f32)
            .astype(bf16)
        )
    item_rows = row_ref[...]
    high = (item_rows >> 6).astype(f32)
    low = (item_rows & 63).astype(f32)
    halves = jnp.concatenate([high, low, jnp.zeros((6, cands), f32)], axis=0).astype(bf16)
    listed = jnp.dot(halves, place[...], preferred_element_type=f32)
    requested = (listed[0:1] * 64.0 + listed[1:2]).astype(jnp.int32)
    for owner in range(groups):
        asked[owner] = requested[:, owner * MOST : (owner + 1) * MOST]

    def ask(peer, slot):
        return pltpu.make_async_remote_copy(
            src_ref=asked.at[peer], dst_ref=wanted.at[slot], send_sem=ask_send.at[peer],
            recv_sem=ask_recv.at[slot], device_id={"grp": peer}, device_id_type=MESH,
        )

    def give_back(peer, slot):
        return pltpu.make_async_remote_copy(
            src_ref=found.at[peer], dst_ref=returned.at[slot], send_sem=back_send.at[peer],
            recv_sem=back_recv.at[slot], device_id={"grp": peer}, device_id_type=MESH,
        )

    @pl.loop(1, groups)
    def _(k):
        ask((me + k) % groups, me).start()

    wanted[me] = asked[me]

    @pl.loop(1, groups)
    def _(k):
        peer = (me + k) % groups
        ask(peer, peer).wait_recv()

    at_once = 4
    chunk = 512

    @pl.loop(0, groups // at_once)
    def _(batch):
        columns = []
        for k in range(at_once):
            line = wanted[batch * at_once + k].astype(f32)
            columns.append(jnp.broadcast_to(line, (MOST, MOST)).T[:, 0:1].astype(jnp.int32))
        column = jnp.concatenate(columns, axis=0)
        total = jnp.zeros((at_once * MOST, D), f32)
        for start in range(0, items, chunk):
            picks = (
                column
                == start + lax.broadcasted_iota(jnp.int32, (at_once * MOST, chunk), 1)
            ).astype(f32).astype(bf16)
            total += jnp.dot(
                picks, table_ref[start : start + chunk, :], preferred_element_type=f32
            )
        found[pl.ds(batch * at_once, at_once)] = total.astype(bf16).reshape(at_once, MOST, D)

        @pl.loop(0, at_once)
        def _(k):
            peer = batch * at_once + k

            @pl.when(peer != me)
            def _():
                give_back(peer, me).start()

    returned[me] = found[me]
    relay(0, 1)

    @pl.loop(1, groups)
    def _(k):
        peer = (me + k) % groups
        give_back(peer, peer).wait_recv()

    def project(layer, start, rows):
        normed = normalize(rows.astype(f32)).astype(bf16)
        projected = silu_of_twice(
            0.5 * jnp.dot(normed, w_in_ref[layer], preferred_element_type=f32)
        )
        gate[pl.ds(start, tile), :] = projected[:, :D]
        queries[pl.ds(start, tile), :] = projected[:, D:].astype(bf16)
        summed[pl.ds(start, tile), :] = jnp.zeros((tile, D), f32)

    @pl.loop(0, cands // tile)
    def _(step):
        start = pl.multiple_of(step * tile, tile)
        rows = jnp.dot(
            place[pl.ds(start, tile), :],
            returned[...].reshape(groups * MOST, D),
            preferred_element_type=f32,
        ).astype(bf16)
        rows_now[pl.ds(start, tile), :] = rows
        project(0, start, rows)

    length = len_ref[0]

    def attend(layer, chip):
        from_sibling(layer, chip).wait_recv()
        for lane in range(2):
            position = (2 * chip + lane) * hist_rows + lax.broadcasted_iota(
                jnp.int32, (hist_rows, D), 0
            )
            values = kv[layer, 2 * chip + lane, :, D:].astype(f32)
            live_values[lane * hist_rows : (lane + 1) * hist_rows, :] = jnp.where(
                position < length, values, 0.0
            ).astype(bf16)

        @pl.loop(0, cands // tile)
        def _(step):
            start = pl.multiple_of(step * tile, tile)
            for head in range(HEADS):
                part = slice(head * HEAD, (head + 1) * HEAD)
                keys = kv[layer, pl.ds(2 * chip, 2), :, part].reshape(2 * hist_rows, HEAD)
                scores = lax.dot_general(
                    queries[pl.ds(start, tile), part], keys, (((1,), (1,)), ((), ())),
                    preferred_element_type=f32,
                )
                weights = silu_of_twice(scores * (0.5 * score_scale)).astype(bf16)
                summed[pl.ds(start, tile), part] += jnp.dot(
                    weights, live_values[:, part], preferred_element_type=f32
                )

    def finish(layer):
        @pl.loop(0, cands // tile)
        def _(step):
            start = pl.multiple_of(step * tile, tile)
            here = pl.ds(start, tile)
            hidden = (normalize(summed[here, :]) * gate[here, :]).astype(bf16)
            rows = (
                rows_now[here, :].astype(f32)
                + jnp.dot(hidden, w_out_ref[layer], preferred_element_type=f32)
            ).astype(bf16)
            if layer + 1 < LAYERS:
                rows_now[here, :] = rows
                project(layer + 1, start, rows)
            else:
                out_ref[here, :] = rows

    own_copies[1].wait()
    attend(0, pos)
    for distance in range(1, chips):
        if distance + 1 < chips:
            relay(0, distance + 1)
        if distance == max(chips - 3, 1):
            pass_on(1, pos)
        at_distance(distance, partial(attend, 0))
    if chips > 1:
        relay(1, 1)
    finish(0)
    attend(1, pos)
    for distance in range(1, chips):
        if distance + 1 < chips:
            relay(1, distance + 1)
        at_distance(distance, partial(attend, 1))
    finish(1)

    for layer in range(LAYERS):
        @pl.loop(0, chips)
        def _(chip):
            @pl.when(goes_right(chip))
            def _():
                to_right(layer, chip).wait_send()

            @pl.when(goes_left(chip))
            def _():
                to_left(layer, chip).wait_send()

            to_sibling(layer, chip).wait_send()

    @pl.loop(1, groups)
    def _(k):
        peer = (me + k) % groups
        ask(peer, peer).wait_send()
        give_back(peer, peer).wait_send()


def body(item_table, cand_owner, cand_row, hist_kv, hist_len, w_in, w_out):
    groups = lax.axis_size("grp")
    cands = cand_row.shape[1]
    hist_rows = hist_kv.shape[2]
    vmem = pl.BlockSpec(memory_space=pltpu.VMEM)
    dma, f32, bf16 = pltpu.SemaphoreType.DMA, jnp.float32, jnp.bfloat16
    chips = groups // 2
    rows = pl.pallas_call(
        partial(kernel, groups),
        out_shape=jax.ShapeDtypeStruct((cands, D), bf16),
        in_specs=[
            pl.BlockSpec(memory_space=pltpu.SMEM), vmem, vmem, vmem,
            pl.BlockSpec(memory_space=pl.ANY), vmem, vmem,
        ],
        out_specs=vmem,
        scratch_shapes=[
            pltpu.VMEM((LAYERS, groups, hist_rows, 2 * D), bf16),
            pltpu.VMEM((cands, groups * MOST), bf16),
            pltpu.VMEM((groups, 1, MOST), jnp.int32),
            pltpu.VMEM((groups, 1, MOST), jnp.int32),
            pltpu.VMEM((groups, MOST, D), bf16),
            pltpu.VMEM((groups, MOST, D), bf16),
            pltpu.VMEM((cands, D), bf16),
            pltpu.VMEM((cands, D), bf16),
            pltpu.VMEM((cands, D), f32),
            pltpu.VMEM((cands, D), f32),
            pltpu.VMEM((2 * hist_rows, D), bf16),
            dma((LAYERS,)),
            dma((LAYERS, chips)),
            dma((LAYERS, chips)),
            dma((LAYERS, chips)),
            dma((LAYERS, chips)),
            dma((LAYERS, chips)),
            dma((groups,)),
            dma((groups,)),
            dma((groups,)),
            dma((groups,)),
        ],
        compiler_params=pltpu.CompilerParams(
            collective_id=0, has_side_effects=True, vmem_limit_bytes=56 * 1024 * 1024
        ),
    )(hist_len, cand_owner[0], cand_row, item_table, hist_kv[:, 0], w_in, w_out)
    return rows[None]


def solution(mesh):
    in_specs = (
        P("grp", None),
        P("req", "grp", None),
        P("req", "grp"),
        P(None, "req", "grp", None),
        P("req"),
        P(),
        P(),
    )
    out_specs = P("req", "grp", None)
    return jax.shard_map(body, mesh=mesh, in_specs=in_specs, out_specs=out_specs, check_vma=False)
```

time: 208 us -> 124 us (0.60)
  Pallas kernels: 0 us -> 119 us
  matrix products: 58.5 us -> 0 us
  local copies, waits for them, and re-layouts: 49.9 us -> 3.97 us
  waiting for transfers between devices: 37.8 us -> 0 us
  other arithmetic: 29.2 us -> 0 us
  blocking collectives: 13.4 us -> 0 us
  between operations: 13.7 us -> 0.66 us
  starting transfers between devices: 3.78 us -> 0 us
    pallas_call x0 -> x1, Pallas kernels: none -> 119 us  [body(): pl.pallas_call(partial(kernel, groups), out_shape=jax.ShapeDtypeStruct((c...]
    dot_general x12 -> x0, matrix products: 58.5 us -> none  [the longest x8 48.8 us: step(): jnp.einsum('hck,khd->chd', weights, value_rows, preferred_element_type=jn...]
    all_to_all x1 -> x0, waiting for transfers between devices: 37.8 us -> none  [body(): lax.all_to_all(found, 'grp', split_axis=0, concat_axis=0, tiled=True)]
    add x8 -> x0, other arithmetic: 18.5 us -> none  [step(): return summed + attended.reshape(cand_rows, D)]
    slice x11 -> x0, local copies, waits for them, and re-layouts: 16.8 us -> none  [the longest x8 14.2 us: step(): key_rows = part_rows[:, :D].reshape(block_rows, HEADS, HEAD)]
    gather x3 -> x0, local copies, waits for them, and re-layouts: 13.5 us -> none  [the longest x1 6.76 us: body(): found = jnp.take(item_table, wanted_flat, axis=0)]
    all_to_all x1 -> x0, blocking collectives: 13.4 us -> none  [body(): lax.all_to_all(requested, 'grp', split_axis=0, concat_axis=0, tiled=True)]
    unnamed x24 -> x1, local copies, waits for them, and re-layouts: 12.7 us -> 2.26 us
  transfers between devices with their start and end apart: 3 -> 0, of which waited for: 1 -> 0; matrix products, arithmetic and copies ran while one was open for 39% -> 0% of each run, Pallas kernels for 0% -> 0%
where the time goes in v1:
time: 124 us
  Pallas kernels  119 us (96%)
  local copies, waits for them, and re-layouts  3.97 us (3%)
    pallas_call x1, Pallas kernels, body(): pl.pallas_call(partial(kernel, groups), out_shape=jax.ShapeDtypeStruct((c...  119 us

profile of v1, /device:TPU:0, one launch (start us, length us, event | category | flops | bytes accessed | tf_op | source)
XLA Modules:
  0.0 123.6 jit_solution(13529455602433331948)
XLA Ops:
  0.7 1.7 %copy.8.owner_ref = s32[1024,1]{1,0:T(8,128)} copy(s32[1024,1]{0,1:T(1,128)} %bitcast.5) | data formatting | bytes 8192 | tf_op jit(solution)/shard_map/squeeze | solution.py:345
  2.4 119.0 %shard_map.73 = bf16[1024,512]{1,0:T(8,128)(2,1)} custom-call(s32[1]{0:T(128)S(6)} %copy.10.len_ref, s32[1024,1]{1,0:T(8,128)} %copy.8.owner_ref, s32[1,1024]{1,0:T(1,128)} %row_ref.1, bf16[4096,512]{1,0:T(8,128)(2,1)} %table_ref.1, bf16[2,256,1024]{2,1,0:T(8,128)(2,1)} %bitcast.4, bf16[2,512,1024]{2,1,0:T(8,128)(2,1)} %w_in_ref.1, ...), custom_call_target="tpu_custom_call" | custom-call | tf_op jit(solution)/shard_map/pallas_call | solution.py:311
  121.3 2.3 %copy.11 = bf16[1,1024,512]{2,1,0:T(8,128)(2,1)} copy(bf16[1,1024,512]{2,1,0:T(8,128)(2,1)} %bitcast.3) | data formatting | bytes 2097152

commit v2 on v1

--- a/solution.py
+++ b/solution.py
@@ -12,6 +12,7 @@
 HEAD = 128
 LAYERS = 2
 MOST = 128
+PARTS = 1
 MESH = pl.DeviceIdType.MESH
 
 score_scale = 0.35
@@ -29,9 +30,9 @@
 
 def kernel(
     groups,
-    len_ref, owner_ref, row_ref, table_ref, hist_ref, w_in_ref, w_out_ref, out_ref,
-    kv, place, asked, wanted, found, returned, rows_now, queries, gate, summed, live_values,
-    own_sem, z_recv, s_recv, r_send, l_send, s_send, ask_send, ask_recv, back_send, back_recv,
+    len_ref, owner_ref, row_ref, table_hbm, hist_ref, w_in_hbm, w_out_hbm, out_ref,
+    table_ref, w_in_ref, w_out_ref, kv, place, asked, wanted, found, returned, rows_now, queries, gate, summed, live_values,
+    load_sem, own_sem, z_recv, s_recv, r_send, l_send, s_send, ask_send, ask_recv, back_send, back_recv,
 ):
     chips = groups // 2
     me = lax.axis_index("grp")
@@ -41,6 +42,7 @@
     items = table_ref.shape[0]
     hist_rows = hist_ref.shape[1]
     tile = 256
+    half = hist_rows // PARTS
     f32, bf16 = jnp.float32, jnp.bfloat16
 
     barrier = pltpu.get_barrier_semaphore()
@@ -55,28 +57,34 @@
         pltpu.make_async_copy(hist_ref.at[layer], kv.at[layer, me], own_sem.at[layer])
         for layer in range(LAYERS)
     ]
-    for copy in own_copies:
+    loads = [
+        pltpu.make_async_copy(far, near, load_sem.at[index])
+        for index, (far, near) in enumerate(
+            [(table_hbm, table_ref), (w_in_hbm, w_in_ref), (w_out_hbm, w_out_ref)]
+        )
+    ]
+    for copy in own_copies + loads:
         copy.start()
     pl.semaphore_wait(barrier, groups - 1)
 
-    def push(layer, chip, lane, target, send, recv):
-        block = kv.at[layer, 2 * chip + lane]
+    def push(layer, chip, lane, part, target, send, recv):
+        block = kv.at[layer, 2 * chip + lane, pl.ds(part * half, half)]
         return pltpu.make_async_remote_copy(
-            src_ref=block, dst_ref=block, send_sem=send.at[layer, chip],
-            recv_sem=recv.at[layer, chip], device_id={"grp": target}, device_id_type=MESH,
-        )
-
-    def to_right(layer, chip):
-        return push(layer, chip, core, me + 2, r_send, z_recv)
-
-    def to_left(layer, chip):
-        return push(layer, chip, core, me - 2, l_send, z_recv)
-
-    def to_sibling(layer, chip):
-        return push(layer, chip, core, sibling, s_send, s_recv)
-
-    def from_sibling(layer, chip):
-        return push(layer, chip, 1 - core, sibling, s_send, s_recv)
+            src_ref=block, dst_ref=block, send_sem=send.at[layer, chip, part],
+            recv_sem=recv.at[layer, chip, part], device_id={"grp": target}, device_id_type=MESH,
+        )
+
+    def to_right(layer, chip, part):
+        return push(layer, chip, core, part, me + 2, r_send, z_recv)
+
+    def to_left(layer, chip, part):
+        return push(layer, chip, core, part, me - 2, l_send, z_recv)
+
+    def to_sibling(layer, chip, part):
+        return push(layer, chip, core, part, sibling, s_send, s_recv)
+
+    def from_sibling(layer, chip, part):
+        return push(layer, chip, 1 - core, part, sibling, s_send, s_recv)
 
     def goes_right(chip):
         return jnp.logical_and(chip <= pos, pos + 1 < chips)
@@ -84,16 +92,16 @@
     def goes_left(chip):
         return jnp.logical_and(chip >= pos, pos > 0)
 
-    def pass_on(layer, chip):
+    def pass_on(layer, chip, part):
         @pl.when(goes_right(chip))
         def _():
-            to_right(layer, chip).start()
+            to_right(layer, chip, part).start()
 
         @pl.when(goes_left(chip))
         def _():
-            to_left(layer, chip).start()
-
-        to_sibling(layer, chip).start()
+            to_left(layer, chip, part).start()
+
+        to_sibling(layer, chip, part).start()
 
     def at_distance(distance, act):
         @pl.loop(0, 2)
@@ -104,17 +112,35 @@
             def _():
                 act(chip)
 
-    def relay(layer, distance):
+    interior = jnp.logical_and(pos > 0, pos + 1 < chips)
+    emitted = set()
+
+    def relay(layer, distance, inner, parts=range(PARTS)):
+        parts = [part for part in parts if (layer, distance, inner, part) not in emitted]
+        if distance >= chips or not parts:
+            return
+        emitted.update((layer, distance, inner, part) for part in parts)
+
         def act(chip):
-            to_right(layer, chip).wait_recv()
-            pass_on(layer, chip)
-
-        at_distance(distance, act)
+            for part in parts:
+                to_right(layer, chip, part).wait_recv()
+                pass_on(layer, chip, part)
+
+        @pl.when(interior if inner else jnp.logical_not(interior))
+        def _():
+            at_distance(distance, act)
 
     own_copies[0].wait()
-    pass_on(0, pos)
-
-    owners = owner_ref[...]
+    for part in range(PARTS):
+        pass_on(0, pos, part)
+
+    owners = jnp.concatenate(
+        [
+            jnp.broadcast_to(owner_ref[:, start : start + 128].astype(f32), (128, 128)).T[:, 0:1]
+            for start in range(0, cands, 128)
+        ],
+        axis=0,
+    ).astype(jnp.int32)
     names = (owners == lax.broadcasted_iota(jnp.int32, (cands, 128), 1)).astype(f32)
     names16 = names.astype(bf16)
     for start in range(0, cands, tile):
@@ -165,8 +191,7 @@
     at_once = 4
     chunk = 512
 
-    @pl.loop(0, groups // at_once)
-    def _(batch):
+    def gather(batch):
         columns = []
         for k in range(at_once):
             line = wanted[batch * at_once + k].astype(f32)
@@ -191,8 +216,18 @@
             def _():
                 give_back(peer, me).start()
 
+    loads[0].wait()
+    for batch in range(groups // at_once):
+        gather(batch)
+        if batch == 0:
+            relay(0, 1, True)
     returned[me] = found[me]
-    relay(0, 1)
+    own_copies[1].wait()
+    for part in range(PARTS):
+        pass_on(1, pos, part)
+    relay(0, 2, True)
+    loads[1].wait()
+    loads[2].wait()
 
     @pl.loop(1, groups)
     def _(k):
@@ -221,14 +256,16 @@
 
     length = len_ref[0]
 
-    def attend(layer, chip):
-        from_sibling(layer, chip).wait_recv()
+    def attend(layer, chip, parts=range(PARTS)):
+        for part in parts:
+            from_sibling(layer, chip, part).wait_recv()
+        first, size = parts[0] * half, len(parts) * half
         for lane in range(2):
-            position = (2 * chip + lane) * hist_rows + lax.broadcasted_iota(
-                jnp.int32, (hist_rows, D), 0
+            position = (2 * chip + lane) * hist_rows + first + lax.broadcasted_iota(
+                jnp.int32, (size, D), 0
             )
-            values = kv[layer, 2 * chip + lane, :, D:].astype(f32)
-            live_values[lane * hist_rows : (lane + 1) * hist_rows, :] = jnp.where(
+            values = kv[layer, 2 * chip + lane, first : first + size, D:].astype(f32)
+            live_values[lane * size : (lane + 1) * size, :] = jnp.where(
                 position < length, values, 0.0
             ).astype(bf16)
 
@@ -236,15 +273,17 @@
         def _(step):
             start = pl.multiple_of(step * tile, tile)
             for head in range(HEADS):
-                part = slice(head * HEAD, (head + 1) * HEAD)
-                keys = kv[layer, pl.ds(2 * chip, 2), :, part].reshape(2 * hist_rows, HEAD)
+                cols = slice(head * HEAD, (head + 1) * HEAD)
+                keys = kv[
+                    layer, pl.ds(2 * chip, 2), first : first + size, cols
+                ].reshape(2 * size, HEAD)
                 scores = lax.dot_general(
-                    queries[pl.ds(start, tile), part], keys, (((1,), (1,)), ((), ())),
+                    queries[pl.ds(start, tile), cols], keys, (((1,), (1,)), ((), ())),
                     preferred_element_type=f32,
                 )
                 weights = silu_of_twice(scores * (0.5 * score_scale)).astype(bf16)
-                summed[pl.ds(start, tile), part] += jnp.dot(
-                    weights, live_values[:, part], preferred_element_type=f32
+                summed[pl.ds(start, tile), cols] += jnp.dot(
+                    weights, live_values[: 2 * size, cols], preferred_element_type=f32
                 )
 
     def finish(layer):
@@ -263,36 +302,41 @@
             else:
                 out_ref[here, :] = rows
 
-    own_copies[1].wait()
+    relay(0, 1, False)
     attend(0, pos)
     for distance in range(1, chips):
-        if distance + 1 < chips:
-            relay(0, distance + 1)
-        if distance == max(chips - 3, 1):
-            pass_on(1, pos)
+        relay(0, distance + 1, True)
+        relay(0, distance + 1, False)
+        relay(1, distance, True)
         at_distance(distance, partial(attend, 0))
-    if chips > 1:
-        relay(1, 1)
+    relay(1, 1, False)
     finish(0)
     attend(1, pos)
     for distance in range(1, chips):
-        if distance + 1 < chips:
-            relay(1, distance + 1)
-        at_distance(distance, partial(attend, 1))
+        relay(1, distance + 1, True)
+        if distance + 1 < chips - 1:
+            relay(1, distance + 1, False)
+        if distance < chips - 1:
+            at_distance(distance, partial(attend, 1))
+            continue
+        for part in range(PARTS):
+            relay(1, distance, False, [part])
+            at_distance(distance, partial(attend, 1, parts=[part]))
     finish(1)
 
     for layer in range(LAYERS):
         @pl.loop(0, chips)
         def _(chip):
-            @pl.when(goes_right(chip))
-            def _():
-                to_right(layer, chip).wait_send()
-
-            @pl.when(goes_left(chip))
-            def _():
-                to_left(layer, chip).wait_send()
-
-            to_sibling(layer, chip).wait_send()
+            for part in range(PARTS):
+                @pl.when(goes_right(chip))
+                def _():
+                    to_right(layer, chip, part).wait_send()
+
+                @pl.when(goes_left(chip))
+                def _():
+                    to_left(layer, chip, part).wait_send()
+
+                to_sibling(layer, chip, part).wait_send()
 
     @pl.loop(1, groups)
     def _(k):
@@ -306,17 +350,20 @@
     cands = cand_row.shape[1]
     hist_rows = hist_kv.shape[2]
     vmem = pl.BlockSpec(memory_space=pltpu.VMEM)
+    far = pl.BlockSpec(memory_space=pl.ANY)
     dma, f32, bf16 = pltpu.SemaphoreType.DMA, jnp.float32, jnp.bfloat16
     chips = groups // 2
     rows = pl.pallas_call(
         partial(kernel, groups),
         out_shape=jax.ShapeDtypeStruct((cands, D), bf16),
         in_specs=[
-            pl.BlockSpec(memory_space=pltpu.SMEM), vmem, vmem, vmem,
-            pl.BlockSpec(memory_space=pl.ANY), vmem, vmem,
+            pl.BlockSpec(memory_space=pltpu.SMEM), vmem, vmem, far, far, far, far,
         ],
         out_specs=vmem,
         scratch_shapes=[
+            pltpu.VMEM(item_table.shape, bf16),
+            pltpu.VMEM(w_in.shape, bf16),
+            pltpu.VMEM(w_out.shape, bf16),
             pltpu.VMEM((LAYERS, groups, hist_rows, 2 * D), bf16),
             pltpu.VMEM((cands, groups * MOST), bf16),
             pltpu.VMEM((groups, 1, MOST), jnp.int32),
@@ -328,12 +375,13 @@
             pltpu.VMEM((cands, D), f32),
             pltpu.VMEM((cands, D), f32),
             pltpu.VMEM((2 * hist_rows, D), bf16),
+            dma((3,)),
             dma((LAYERS,)),
-            dma((LAYERS, chips)),
-            dma((LAYERS, chips)),
-            dma((LAYERS, chips)),
-            dma((LAYERS, chips)),
-            dma((LAYERS, chips)),
+            dma((LAYERS, chips, PARTS)),
+            dma((LAYERS, chips, PARTS)),
+            dma((LAYERS, chips, PARTS)),
+            dma((LAYERS, chips, PARTS)),
+            dma((LAYERS, chips, PARTS)),
             dma((groups,)),
             dma((groups,)),
             dma((groups,)),
@@ -342,7 +390,7 @@
         compiler_params=pltpu.CompilerParams(
             collective_id=0, has_side_effects=True, vmem_limit_bytes=56 * 1024 * 1024
         ),
-    )(hist_len, cand_owner[0], cand_row, item_table, hist_kv[:, 0], w_in, w_out)
+    )(hist_len, cand_owner[:, :, 0], cand_row, item_table, hist_kv[:, 0], w_in, w_out)
     return rows[None]
 
 

time: 124 us -> 115 us (0.927)
  Pallas kernels: 119 us -> 111 us
  local copies, waits for them, and re-layouts: 3.97 us -> 2.26 us
    pallas_call x1, Pallas kernels: 119 us -> 111 us  [body(): pl.pallas_call(partial(kernel, groups), out_shape=jax.ShapeDtypeStruct((c...]
    squeeze x1 -> x0, local copies, waits for them, and re-layouts: 1.71 us -> none  [body(): cand_owner[0]]
where the time goes in v2:
time: 115 us; the launch traced here: 114 us
  Pallas kernels  111 us (97%)
  local copies, waits for them, and re-layouts  2.26 us (2%)
    pallas_call x1, Pallas kernels, body(): pl.pallas_call(partial(kernel, groups), out_shape=jax.ShapeDtypeStruct((c...  111 us

profile of v2, /device:TPU:0, one launch (start us, length us, event | category | flops | bytes accessed | tf_op | source)
XLA Modules:
  0.0 114.0 jit_solution(5396965792340363690)
XLA Ops:
  0.7 111.1 %shard_map.73 = bf16[1024,512]{1,0:T(8,128)(2,1)} custom-call(s32[1]{0:T(128)S(6)} %copy.9.len_ref, s32[1,1024]{1,0:T(1,128)} %bitcast.5, s32[1,1024]{1,0:T(1,128)} %row_ref.1, bf16[4096,512]{1,0:T(8,128)(2,1)} %table_hbm.1, bf16[2,256,1024]{2,1,0:T(8,128)(2,1)} %bitcast.4, bf16[2,512,1024]{2,1,0:T(8,128)(2,1)} %w_in_hbm.1, bf16[2,512,512]{2,1,0:T(8,128)(2,1)} %w_out_hbm.1), custom_call_target="tpu_custom_call" | custom-call | tf_op jit(solution)/shard_map/pallas_call | solution.py:356
  111.7 2.3 %copy.10 = bf16[1,1024,512]{2,1,0:T(8,128)(2,1)} copy(bf16[1,1024,512]{2,1,0:T(8,128)(2,1)} %bitcast.3) | data formatting | bytes 2097152
